TPU v7x, 32 devices: a whole 2x2x4 slice. The times are simulated.
32 devices in a mesh: parts: 2 (over y), tensor: 4 (over z), dp: 4 (over x, core).
Axes of the slice: x: 2, y: 2, z: 4, core: 2. Of those that a mesh axis runs over, the one named last changes fastest.
Arguments:
- inputs: bfloat16 [4096, 8192], P(('parts', 'dp'), 'tensor'), parts along dimension 0, may hold values from -6 to 6
- cotangent: bfloat16 [4096, 8192], P(('parts', 'dp'), 'tensor'), parts along dimension 0, may hold values from -6 to 6
- weight: bfloat16 [8192, 8192], P(None, 'tensor'), may hold values from -0.0625 to 0.0625
- down_weight_maps: bfloat16 [8192, 2048], P('tensor', 'parts'), parts along dimension 1, may hold values from -0.0625 to 0.0625
- up_weight_maps: bfloat16 [2048, 8192], P('parts', 'tensor'), parts along dimension 0, may hold values from -0.75 to 0.75
- counts: int32 [8, 16], P('parts'), parts along dimension 0, may hold values from 0 to 256, as said below
- ranks: int32 [32], P('parts'), parts along dimension 0, may hold values from 8 to 64, as said below
- owners: int32 [32], P('parts'), parts along dimension 0, may hold values from 0 to 3
Outputs:
- projected: bfloat16 [4096, 8192], P(('parts', 'dp'), 'tensor'), parts along dimension 0
- input_grad: bfloat16 [4096, 8192], P(('parts', 'dp'), 'tensor'), parts along dimension 0
- grad_a: float32 [8, 8192, 1024], P(('parts', 'dp'), 'tensor'), parts along dimension 0
- grad_b: float32 [8, 1024, 8192], P(('parts', 'dp'), None, 'tensor'), parts along dimension 0
There are 2 independent parts, one for each index of `parts`. A program takes and returns all parts, laid end to end along the dimension named above; an argument that names none is the same for every part. Nothing has to cross between parts.
Inputs may be any that keep to these rules, and one draw needn't show every extreme that they name: `counts`: each row sums to at most 512, one row to exactly 512, and all rows together to exactly 1024; some entry is exactly 256. `ranks`: each rank is 64 divided by 1, 2, 4 or 8; some trial has 64 and some 64 // 8.
All inputs are finite; a program needn't handle non-finite values.
Results may differ from a plain program's by a relative error of at most 0.0034.
Values may be sent and summed in bfloat16 or wider, within the bound.
A program may use at most 256 MiB of HBM per device.

v0:
```python
import jax
import jax.numpy as jnp
from jax import lax
from jax.sharding import PartitionSpec as P

LARGEST_RANK = 64
TRIALS = 16
LANES = 128
adapter_alpha = 16.0
TRAILING = (((1,), (1,)), ((), ()))
FIRST = (((0,), (0,)), ((), ()))


def fold_columns(values, match):
    width = values.shape[1]
    kept = jnp.where(match, values, 0.0)
    return sum((kept[:, i : i + LANES] for i in range(0, width, LANES)))


def spread_columns(folded, match):
    repeats = match.shape[1] // LANES
    return jnp.where(
        match, jnp.concatenate([folded] * repeats, axis=1), jnp.zeros((), folded.dtype)
    )


def local(inputs, cotangent, weight, down_weight_maps, up_weight_maps, counts, ranks, owners):
    slot_count, feature_local = inputs.shape
    group_count = counts.shape[0]
    width = down_weight_maps.shape[1]
    column = jnp.arange(width, dtype=jnp.int32)
    col_trial = column // LARGEST_RANK
    column_slot = column % LARGEST_RANK
    trial_ids = jnp.arange(TRIALS, dtype=jnp.int32)
    matches = col_trial[:, None] == trial_ids[None, :]
    rank_per_column = jnp.sum(jnp.where(matches, ranks[None, :], 0), axis=1)
    owner_col = jnp.sum(jnp.where(matches, owners[None, :], 0), axis=1)
    scale_per_column = jnp.where(
        column_slot < rank_per_column, adapter_alpha / rank_per_column.astype(jnp.float32), 0.0
    )
    trial_rows = jnp.sum(counts, axis=0)
    per_trial = 1.0 / jnp.maximum(trial_rows, 1).astype(jnp.float32)
    inverse_col = jnp.sum(jnp.where(matches, per_trial[None, :], 0.0), axis=1)
    cumulative = jnp.cumsum(counts, axis=1)
    group_ids = jnp.arange(group_count, dtype=jnp.int32)
    my_group = lax.axis_index("dp")
    positions = jnp.arange(slot_count, dtype=jnp.int32)
    trial_all = jnp.sum(
        (positions[None, :, None] >= cumulative[:, None, :]).astype(jnp.int32), axis=2
    )
    row_trial = jnp.sum(jnp.where((group_ids == my_group)[:, None], trial_all, 0), axis=0)
    is_live = row_trial < TRIALS
    match = row_trial[:, None] == col_trial[None, :]
    match_all = trial_all.reshape(-1)[:, None] == col_trial[None, :]
    coef = jnp.where(match, scale_per_column[None, :], 0.0)
    coef_folded = fold_columns(coef, match)
    down_part = jnp.dot(inputs, down_weight_maps, preferred_element_type=jnp.float32)
    back_part = lax.dot_general(
        cotangent, up_weight_maps, TRAILING, preferred_element_type=jnp.float32
    )
    folded = jnp.concatenate(
        [fold_columns(down_part, match), fold_columns(back_part, match)], axis=1
    )
    folded = lax.psum(folded, "tensor")
    scaled_down_f = (coef_folded * folded[:, :LANES]).astype(jnp.bfloat16)
    scaled_back_f = (coef_folded * folded[:, LANES:]).astype(jnp.bfloat16)
    all_inputs = lax.all_gather(inputs, "tensor", axis=1, tiled=True)
    mine = lax.axis_index("tensor")
    block = jnp.arange(weight.shape[0], dtype=jnp.int32) // feature_local
    frozen_back = lax.dot_general(cotangent, weight, TRAILING, preferred_element_type=jnp.float32)
    others = jnp.where((block == mine)[None, :], 0.0, frozen_back).astype(jnp.bfloat16)
    others_share = lax.psum_scatter(others, "tensor", scatter_dimension=1, tiled=True)
    own_weight = lax.dynamic_slice_in_dim(weight, mine * feature_local, feature_local, 0)
    own_share = lax.dot_general(cotangent, own_weight, TRAILING, preferred_element_type=jnp.float32)
    frozen_share = own_share + others_share.astype(jnp.float32)
    group_inputs = lax.all_gather(inputs, "dp", axis=0, tiled=True)
    group_cotangent = lax.all_gather(cotangent, "dp", axis=0, tiled=True)
    both = lax.all_gather(
        jnp.concatenate([scaled_down_f, scaled_back_f], axis=1), "dp", axis=0, tiled=True
    )
    frozen_output = jnp.dot(all_inputs, weight, preferred_element_type=jnp.float32)
    scaled_down = spread_columns(scaled_down_f, match)
    scaled_back = spread_columns(scaled_back_f, match)
    merged = frozen_output + jnp.dot(
        scaled_down, up_weight_maps, preferred_element_type=jnp.float32
    )
    projected = jnp.where(is_live[:, None], merged, 0.0).astype(jnp.bfloat16)
    adapter_in = lax.dot_general(
        scaled_back, down_weight_maps, TRAILING, preferred_element_type=jnp.float32
    )
    input_grad = jnp.where(is_live[:, None], frozen_share + adapter_in, 0.0).astype(jnp.bfloat16)
    owned = jnp.where(owner_col == my_group, inverse_col, 0.0)
    down_all = spread_columns(both[:, :LANES], match_all)
    back_all = spread_columns(both[:, LANES:], match_all)
    grad_a = lax.dot_general(group_inputs, back_all, FIRST, preferred_element_type=jnp.float32)
    grad_b = lax.dot_general(down_all, group_cotangent, FIRST, preferred_element_type=jnp.float32)
    grad_a = (grad_a * owned[None, :])[None]
    grad_b = (grad_b * owned[:, None])[None]
    return (projected, input_grad, grad_a, grad_b)


def solution(mesh):
    return jax.shard_map(
        local,
        mesh=mesh,
        in_specs=(
            P(("parts", "dp"), "tensor"),
            P(("parts", "dp"), "tensor"),
            P(None, "tensor"),
            P("tensor", "parts"),
            P("parts", "tensor"),
            P("parts", None),
            P("parts"),
            P("parts"),
        ),
        out_specs=(
            P(("parts", "dp"), "tensor"),
            P(("parts", "dp"), "tensor"),
            P(("parts", "dp"), "tensor", None),
            P(("parts", "dp"), None, "tensor"),
        ),
        check_vma=False,
    )
```

profile of v0, /device:TPU:0, one launch (start us, length us, event | category | flops | bytes accessed | tf_op | source)
XLA Modules:
  0.0 511.5 jit_solution(14548352022868119628)
XLA Ops:
  7.2 0.9 reduce_window_sum.11
  8.3 5.3 %compare_select_fusion.4 = f32[512,1024]{1,0:T(8,128)S(1)} fusion(bf16[512,2048]{1,0:T(8,128)(2,1)} %param.9, bf16[1024,2048]{1,0:T(8,128)(2,1)} %param.12, s32[1024]{0:T(1024)S(1)} %add_select_fusion.1, s32[512]{0:T(512)S(1)} %select_reduce_fusion.3), kind=kOutput, calls=%fused_computation.9 | convolution fusion | flops 2148532224 | bytes 8394752 | tf_op jit(solution)/shard_map/dot_general | solution.py:58
  13.8 2.3 compare_select_fusion.5
  16.2 0.8 pad_maximum_fusion
  17.6 40.7 %all-reduce.2.cloned.1.call-done = f32[512,256]{1,0:T(8,128)} async-done(((f32[512,256]{1,0:T(8,128)}), f32[512,256]{1,0:T(8,128)}) %all-reduce.2.cloned.1.call-update) | async-done | bytes 524304 | tf_op jit(solution)/shard_map/psum | solution.py:64
  58.2 1.1 constant_dynamic-update-slice_fusion.15
  59.3 1.8 constant_dynamic-update-slice_fusion.7
  64.0 24.4 %select_convert_fusion = bf16[512,8192]{1,0:T(8,128)(2,1)} fusion(bf16[512,2048]{1,0:T(8,128)(2,1)S(1)} %copy-done.2, bf16[8192,2048]{1,0:T(8,128)(2,1)} %param.10, pred[8192]{0:T(1024)(128)(4,1)S(1)} %fusion.23), kind=kOutput, calls=%fused_computation | convolution fusion | flops 17188257792 | bytes 44048384 | tf_op jit(solution)/shard_map/dot_general | solution.py:70
  89.6 7.7 %fusion.14 = f32[512,2048]{1,0:T(8,128)} fusion(bf16[2048,1024]{1,0:T(8,128)(2,1)} %param.11, bf16[512,1024]{1,0:T(8,128)(2,1)S(1)} %constant_dynamic-update-slice_fusion.8, s32[1024]{0:T(1024)S(1)} %add_select_fusion.1, s32[512]{0:T(512)S(1)} %select_reduce_fusion.3), kind=kOutput, calls=%fused_computation.25 | convolution fusion | flops 2148532224 | bytes 9443328 | tf_op jit(solution)/shard_map/dot_general | solution.py:88
  97.6 4.4 fusion.13
  102.0 2.0 slice_dynamic-update-slice_fusion.6
  104.0 2.0 slice_dynamic-update-slice_fusion.5
  106.0 1.9 slice_dynamic-update-slice_fusion.4
  107.9 1.9 slice_dynamic-update-slice_fusion.3
  109.8 0.9 slice_dynamic-update-slice_fusion.2
  110.6 0.9 slice_dynamic-update-slice_fusion.1
  111.5 0.9 slice_dynamic-update-slice_fusion
  112.4 1.0 slice_dynamic-update-slice_fusion.7
  113.4 0.8 slice_dynamic-update-slice_fusion.13
  114.3 0.8 slice_dynamic-update-slice_fusion.12
  115.1 0.8 slice_dynamic-update-slice_fusion.11
  115.9 0.8 slice_dynamic-update-slice_fusion.10
  116.8 0.8 slice_dynamic-update-slice_fusion.9
  119.2 19.4 %all-gather.9.cloned.1.call-done = bf16[2048,2048]{1,0:T(8,128)(2,1)} async-done(((bf16[512,2048]{1,0:T(8,128)(2,1)}), bf16[2048,2048]{1,0:T(8,128)(2,1)}) %all-gather.9.cloned.1.call-update) | async-done | bytes 8388624 | tf_op jit(solution)/shard_map/all_gather | solution.py:76
  138.6 14.9 %multiply_bitcast_fusion.1 = f32[1,2048,1024]{1,2,0:T(8,128)} fusion(bf16[2048,2048]{1,0:T(8,128)(2,1)} %all-gather.9.cloned.1.call-done, bf16[2048,1024]{1,0:T(8,128)(2,1)} %slice_dynamic-update-slice_fusion.15, f32[1024]{0:T(1024)S(1)} %compare_select_fusion.12, s32[1024]{0:T(1024)S(1)} %add_select_fusion.1, s32[2048]{0:T(1024)S(1)} %bitcast.30), kind=kOutput, calls=%fused_computation.4 | convolution fusion | flops 8596226048 | bytes 20987904 | tf_op jit(solution)/shard_map/dot_general | solution.py:95
  153.5 9.2 %copy.15 = f32[1,2048,1024]{2,1,0:T(8,128)} copy(f32[1,2048,1024]{1,2,0:T(8,128)} %multiply_bitcast_fusion.1) | data formatting | bytes 16777216
  162.7 35.6 %all-gather.11.cloned.1.call-done = bf16[2048,2048]{1,0:T(8,128)(2,1)} async-done(((bf16[512,2048]{1,0:T(8,128)(2,1)}), bf16[2048,2048]{1,0:T(8,128)(2,1)}) %all-gather.11.cloned.1.call-update) | async-done | bytes 8388624 | tf_op jit(solution)/shard_map/all_gather | solution.py:77
  198.3 14.9 %multiply_bitcast_fusion = f32[1,1024,2048]{2,1,0:T(8,128)} fusion(bf16[2048,2048]{1,0:T(8,128)(2,1)} %all-gather.11.cloned.1.call-done, bf16[2048,1024]{1,0:T(8,128)(2,1)} %get-tuple-element.19, f32[1024]{0:T(1024)S(1)} %compare_select_fusion.12, s32[1024]{0:T(1024)S(1)} %add_select_fusion.1, s32[2048]{0:T(1024)S(1)} %bitcast.31), kind=kOutput, calls=%fused_computation.3 | convolution fusion | flops 8596226048 | bytes 20987904 | tf_op jit(solution)/shard_map/dot_general | solution.py:96
  213.2 136.2 %all-gather.5.cloned.1.call-done = bf16[512,8192]{1,0:T(8,128)(2,1)} async-done(((bf16[512,2048]{1,0:T(8,128)(2,1)}), bf16[512,8192]{1,0:T(8,128)(2,1)}) %all-gather.5.cloned.1.call-update) | async-done | bytes 8388624 | tf_op jit(solution)/shard_map/all_gather | solution.py:67
  349.4 24.9 %select_convert_fusion.1 = bf16[512,2048]{1,0:T(8,128)(2,1)} fusion(f32[512,2048]{1,0:T(8,128)} %fusion.13, bf16[512,8192]{1,0:T(8,128)(2,1)} %all-gather.5.cloned.1.call-done, bf16[8192,2048]{1,0:T(8,128)(2,1)} %param.10, pred[512]{0:T(512)(128)(4,1)S(1)} %broadcast_compare_fusion), kind=kOutput, calls=%fused_computation.19 | convolution fusion | flops 17183014912 | bytes 48235008 | tf_op jit(solution)/shard_map/dot_general | solution.py:81
  374.3 120.0 %reduce-scatter.2.cloned.1.call-done = bf16[512,2048]{1,0:T(8,128)(2,1)} async-done(((bf16[512,8192]{1,0:T(8,128)(2,1)}), bf16[512,2048]{1,0:T(8,128)(2,1)}) %reduce-scatter.2.cloned.1.call-update) | async-done | bytes 2097168 | tf_op jit(solution)/shard_map/reduce_scatter | solution.py:72
  494.3 10.3 %fusion.4 = bf16[512,2048]{1,0:T(8,128)(2,1)} fusion(f32[512,2048]{1,0:T(8,128)} %fusion.14, bf16[512,2048]{1,0:T(8,128)(2,1)} %reduce-scatter.2.cloned.1.call-done, bf16[512,2048]{1,0:T(8,128)(2,1)S(1)} %copy-done.2, bf16[8192,2048]{1,0:T(8,128)(2,1)} %param.10, s32[]{:T(128)S(6)} %select_n.128, pred[512]{0:T(512)(128)(4,1)S(1)} %broadcast_compare_fusion), kind=kOutput, calls=%fused_computation.16 | convolution fusion | flops 4300210176 | bytes 18874884 | tf_op jit(solution)/shard_map/dot_general | solution.py:74
  (64 shorter events, 6.7 us)
Async XLA Ops:
  7.2 51.1 %all-reduce.2.cloned.1.call-start = ((), (), s32[]{:S(2)}) async-start(), calls=%async_computation.2 | async-start | bytes 1048576 | tf_op jit(solution)/shard_map/psum | solution.py:64
  8.3 5.5 %copy-start.1 = (bf16[512,2048]{1,0:T(8,128)(2,1)S(1)}, bf16[512,2048]{1,0:T(8,128)(2,1)}, u32[]{:S(2)}) copy-start(bf16[512,2048]{1,0:T(8,128)(2,1)} %param.8) | copy-start | bytes 6291460
  8.3 5.5 %copy-start.7 = (bf16[2048,1024]{1,0:T(8,128)(2,1)S(1)}, bf16[2048,1024]{1,0:T(8,128)(2,1)}, u32[]{:S(2)}) copy-start(bf16[2048,1024]{1,0:T(8,128)(2,1)} %param.11) | copy-start | bytes 12582916
  13.8 3.4 copy-start.5
  13.8 3.4 copy-start.6
  17.1 84.9 %all-gather.7.cloned.1.call-start = ((), (), s32[]{:S(2)}) async-start(), calls=%async_computation.4 | async-start | bytes 1310720 | tf_op jit(solution)/shard_map/all_gather | solution.py:78
  59.3 4.7 copy-start.2
  61.8 76.8 %all-gather.9.cloned.1.call-start = ((), (), s32[]{:S(2)}) async-start(), calls=%async_computation.5 | async-start | bytes 10485760 | tf_op jit(solution)/shard_map/all_gather | solution.py:76
  62.6 135.8 %all-gather.11.cloned.1.call-start = ((), (), s32[]{:S(2)}) async-start(), calls=%async_computation.6 | async-start | bytes 10485760 | tf_op jit(solution)/shard_map/all_gather | solution.py:77
  63.2 286.3 %all-gather.5.cloned.1.call-start = ((), (), s32[]{:S(2)}) async-start(), calls=%async_computation.1 | async-start | bytes 10485760 | tf_op jit(solution)/shard_map/all_gather | solution.py:67
  63.8 430.6 %reduce-scatter.2.cloned.1.call-start = ((), (), s32[]{:S(2)}) async-start(), calls=%async_computation.3 | async-start | bytes 10485760 | tf_op jit(solution)/shard_map/reduce_scatter | solution.py:72
  88.4 0.7 copy-start.4
  89.5 7.7 %copy-start.3 = (bf16[512,1024]{1,0:T(8,128)(2,1)S(1)}, bf16[512,1024]{1,0:T(8,128)(2,1)}, u32[]{:S(2)}) copy-start(bf16[512,1024]{1,0:T(8,128)(2,1)} %get-tuple-element.17) | copy-start | bytes 3145732
  89.5 8.0 %copy-start.8 = (bf16[1024,2048]{1,0:T(8,128)(2,1)S(1)}, bf16[1024,2048]{1,0:T(8,128)(2,1)}, u32[]{:S(2)}) copy-start(bf16[1024,2048]{1,0:T(8,128)(2,1)} %param.12) | copy-start | bytes 12582916
  102.0 7.8 %copy-start = (bf16[2048,256]{1,0:T(8,128)(2,1)S(1)}, bf16[2048,256]{1,0:T(8,128)(2,1)}, u32[]{:S(2)}) copy-start(bf16[2048,256]{1,0:T(8,128)(2,1)} %all-gather.7.cloned.1.call-done) | copy-start | bytes 3145732
Sparse Core Ops, SparseCore 0:
  17.2 40.9 all-reduce.1
  62.0 16.6 all-gather.6
  80.3 58.2 all-gather.8
  140.0 58.2 all-gather.10
  199.8 149.6 all-gather.4
  351.6 142.6 reduce-scatter.1
where the time goes:
time: 512 us; the launch traced here: 511 us
  waiting for transfers between devices  354 us (69%)
  matrix products  109 us (21%)
  local copies, waits for them, and re-layouts  27.7 us (5%)
  between operations  14.4 us (3%)
  other arithmetic  6.18 us (1%)
    all_gather x1, waiting for transfers between devices, local(): all_inputs = lax.all_gather(inputs, 'tensor', axis=1, tiled=True)  136 us
    reduce_scatter x1, waiting for transfers between devices, local(): lax.psum_scatter(others, 'tensor', scatter_dimension=1, tiled=True)  120 us
    psum x1, waiting for transfers between devices, local(): folded = lax.psum(folded, 'tensor')  40.7 us
    all_gather x1, waiting for transfers between devices, local(): group_cotangent = lax.all_gather(cotangent, 'dp', axis=0, tiled=True)  35.6 us
    unnamed x45, local copies, waits for them, and re-layouts  25.8 us
    dot_general x1, matrix products, local(): jnp.dot(all_inputs, weight, preferred_element_type=jnp.float32)  24.9 us
    dot_general x1, matrix products, local(): lax.dot_general(cotangent, weight, TRAILING, preferred_element_type=jnp.f...  24.4 us
    all_gather x1, waiting for transfers between devices, local(): group_inputs = lax.all_gather(inputs, 'dp', axis=0, tiled=True)  19.4 us
  transfers between devices with their start and end apart: 6, of which 5 were waited for; matrix products, arithmetic and copies ran while one was open for 23% of the time, Pallas kernels for 0%

commit v1 on v0

--- a/solution.py
+++ b/solution.py
@@ -9,6 +9,19 @@
 adapter_alpha = 16.0
 TRAILING = (((1,), (1,)), ((), ()))
 FIRST = (((0,), (0,)), ((), ()))
+
+
+def shelves_extend(q_in):
+    nd = lax.axis_size("dp")
+    fields = tuple(((m, (m + 1) % nd) for m in range(nd)))
+
+    def begin_records(a_next):
+        if len(a_next) == nd:
+            return a_next
+        return begin_records([lax.ppermute(a_next[0], "dp", fields), *a_next])
+
+    res = jnp.concatenate(begin_records([q_in]), axis=0)
+    return jnp.roll(res, (lax.axis_index("dp") + 1) * q_in.shape[0], axis=0)
 
 
 def fold_columns(values, match):
@@ -73,7 +86,7 @@
     own_weight = lax.dynamic_slice_in_dim(weight, mine * feature_local, feature_local, 0)
     own_share = lax.dot_general(cotangent, own_weight, TRAILING, preferred_element_type=jnp.float32)
     frozen_share = own_share + others_share.astype(jnp.float32)
-    group_inputs = lax.all_gather(inputs, "dp", axis=0, tiled=True)
+    group_inputs = shelves_extend(inputs)
     group_cotangent = lax.all_gather(cotangent, "dp", axis=0, tiled=True)
     both = lax.all_gather(
         jnp.concatenate([scaled_down_f, scaled_back_f], axis=1), "dp", axis=0, tiled=True

time: 512 us -> 471 us (0.920)
  waiting for transfers between devices: 354 us -> 320 us
  local copies, waits for them, and re-layouts: 27.7 us -> 20.1 us
    ppermute x0 -> x3, waiting for transfers between devices: none -> 73.3 us  [begin_records(): return begin_records([lax.ppermute(a_next[0], 'dp', fields), *a_next])]
    all_gather x1, waiting for transfers between devices: 136 us -> 85.7 us  [local(): all_inputs = lax.all_gather(inputs, 'tensor', axis=1, tiled=True)]
    all_gather x1, waiting for transfers between devices: 35.6 us -> 0.01 us  [local(): group_cotangent = lax.all_gather(cotangent, 'dp', axis=0, tiled=True)]
    all_gather x1 -> x0, waiting for transfers between devices: 19.4 us -> none  [local(): group_inputs = lax.all_gather(inputs, 'dp', axis=0, tiled=True)]
    unnamed x45 -> x53, local copies, waits for them, and re-layouts: 25.8 us -> 18.8 us
  transfers between devices with their start and end apart: 6 -> 8, of which waited for: 5 -> 5; matrix products, arithmetic and copies ran while one was open for 23% -> 23% of each run, Pallas kernels for 0% -> 0%
where the time goes in v1:
time: 471 us; the launch traced here: 470 us
  waiting for transfers between devices  320 us (68%)
  matrix products  106 us (23%)
  local copies, waits for them, and re-layouts  20.1 us (4%)
  between operations  14.2 us (3%)
  other arithmetic  8.02 us (2%)
    reduce_scatter x1, waiting for transfers between devices, local(): lax.psum_scatter(others, 'tensor', scatter_dimension=1, tiled=True)  120 us
    all_gather x1, waiting for transfers between devices, local(): all_inputs = lax.all_gather(inputs, 'tensor', axis=1, tiled=True)  85.7 us
    ppermute x3, waiting for transfers between devices, begin_records(): return begin_records([lax.ppermute(a_next[0], 'dp', fields), *a_next])  73.3 us
    psum x1, waiting for transfers between devices, local(): folded = lax.psum(folded, 'tensor')  39.4 us
    dot_general x1, matrix products, local(): lax.dot_general(cotangent, weight, TRAILING, preferred_element_type=jnp.f...  25 us
    dot_general x1, matrix products, local(): jnp.dot(all_inputs, weight, preferred_element_type=jnp.float32)  24.9 us
    unnamed x53, local copies, waits for them, and re-layouts  18.8 us
    dot_general x1, matrix products, local(): lax.dot_general(down_all, group_cotangent, FIRST, preferred_element_type=...  14.9 us
  transfers between devices with their start and end apart: 8, of which 5 were waited for; matrix products, arithmetic and copies ran while one was open for 23% of the time, Pallas kernels for 0%

profile of v1, /device:TPU:0, one launch (start us, length us, event | category | flops | bytes accessed | tf_op | source)
XLA Modules:
  0.0 470.2 jit_solution(5923374684088605973)
XLA Ops:
  7.2 0.9 reduce_window_sum.11
  8.3 5.3 %compare_select_fusion.4 = f32[512,1024]{1,0:T(8,128)S(1)} fusion(bf16[512,2048]{1,0:T(8,128)(2,1)} %param.9, bf16[1024,2048]{1,0:T(8,128)(2,1)} %param.12, s32[1024]{0:T(1024)S(1)} %add_select_fusion.1, s32[512]{0:T(512)S(1)} %select_reduce_fusion.3), kind=kOutput, calls=%fused_computation.11 | convolution fusion | flops 2148532224 | bytes 8394752 | tf_op jit(solution)/shard_map/dot_general | solution.py:71
  13.8 2.3 compare_select_fusion.5
  16.2 0.8 pad_maximum_fusion
  17.3 1.6 compare_select_fusion.6
  18.9 39.4 %all-reduce.2.cloned.1.call-done = f32[512,256]{1,0:T(8,128)} async-done(((f32[512,256]{1,0:T(8,128)}), f32[512,256]{1,0:T(8,128)}) %all-reduce.2.cloned.1.call-update) | async-done | bytes 524304 | tf_op jit(solution)/shard_map/psum | solution.py:77
  58.2 1.7 constant_dynamic-update-slice_fusion.15
  60.0 1.6 constant_dynamic-update-slice_fusion.7
  61.6 0.7 pad_maximum_fusion.1
  62.4 0.7 all-gather.8.cloned.1.call-update
  64.0 25.0 %select_convert_fusion = bf16[512,8192]{1,0:T(8,128)(2,1)} fusion(bf16[512,2048]{1,0:T(8,128)(2,1)} %param.9, bf16[8192,2048]{1,0:T(8,128)(2,1)} %param.10, pred[8192]{0:T(1024)(128)(4,1)S(1)} %fusion.27), kind=kOutput, calls=%fused_computation | convolution fusion | flops 17188257792 | bytes 44048384 | tf_op jit(solution)/shard_map/dot_general | solution.py:83
  89.8 0.7 constant_dynamic-update-slice_fusion.6
  90.5 0.7 constant_dynamic-update-slice_fusion.5
  94.8 7.3 %fusion.17 = f32[512,2048]{1,0:T(8,128)} fusion(bf16[1024,2048]{1,0:T(8,128)(2,1)} %param.12, bf16[512,1024]{1,0:T(8,128)(2,1)} %constant_dynamic-update-slice_fusion, s32[1024]{0:T(1024)S(1)} %add_select_fusion.1, s32[512]{0:T(512)S(1)} %select_reduce_fusion.3), kind=kOutput, calls=%fused_computation.26 | convolution fusion | flops 2148532224 | bytes 9443328 | tf_op jit(solution)/shard_map/dot_general | solution.py:97
  102.1 4.4 fusion.18
  106.6 1.4 collective-permute-start.1
  108.0 1.3 slice_dynamic-update-slice_fusion.6
  109.2 1.2 slice_dynamic-update-slice_fusion.5
  110.5 1.2 slice_dynamic-update-slice_fusion.4
  111.7 1.2 slice_dynamic-update-slice_fusion.3
  114.2 48.6 %collective-permute-done.1 = bf16[512,2048]{1,0:T(8,128)(2,1)} collective-permute-done((bf16[512,2048]{1,0:T(8,128)(2,1)}, bf16[512,2048]{1,0:T(8,128)(2,1)}, u32[]{:S(2)}, u32[]{:S(2)}) %collective-permute-start.1) | collective-permute-done | bytes 2097184 | tf_op jit(solution)/shard_map/ppermute | solution.py:21
  163.7 24.7 %collective-permute-done.2 = bf16[512,2048]{1,0:T(8,128)(2,1)S(1)} collective-permute-done((bf16[512,2048]{1,0:T(8,128)(2,1)}, bf16[512,2048]{1,0:T(8,128)(2,1)S(1)}, u32[]{:S(2)}, u32[]{:S(2)}) %collective-permute-start.2) | collective-permute-done | bytes 2097184 | tf_op jit(solution)/shard_map/ppermute | solution.py:21
  188.6 1.7 constant_dynamic-update-slice_fusion.22
  190.3 1.7 constant_dynamic-update-slice_fusion.21
  192.4 1.7 constant_dynamic-update-slice_fusion.18
  194.1 1.7 constant_dynamic-update-slice_fusion.17
  196.0 11.8 %multiply_bitcast_fusion.1 = f32[1,2048,1024]{2,1,0:T(8,128)} fusion(bf16[4096,2048]{1,0:T(8,128)(2,1)S(1)} %constant_dynamic-update-slice_fusion.16, s32[]{:T(128)S(6)} %select_n.146, bf16[2048,1024]{1,0:T(8,128)(2,1)S(1)} %slice_dynamic-update-slice_fusion.15, f32[1024]{0:T(1024)S(1)} %compare_select_fusion.12, s32[1024]{0:T(1024)S(1)} %add_select_fusion.1, ...), kind=kOutput, calls=%fused_computation.4 | convolution fusion | flops 8596226048 | bytes 20987908 | tf_op jit(solution)/shard_map/dot_general | solution.py:108
  207.8 14.9 %multiply_bitcast_fusion = f32[1,1024,2048]{2,1,0:T(8,128)} fusion(bf16[2048,2048]{1,0:T(8,128)(2,1)} %all-gather.8.cloned.1.call-done, bf16[2048,1024]{1,0:T(8,128)(2,1)} %copy-done.4, f32[1024]{0:T(1024)S(1)} %compare_select_fusion.12, s32[1024]{0:T(1024)S(1)} %add_select_fusion.1, s32[2048]{0:T(1024)S(1)} %bitcast.28), kind=kOutput, calls=%fused_computation.3 | convolution fusion | flops 8596226048 | bytes 20987904 | tf_op jit(solution)/shard_map/dot_general | solution.py:109
  222.7 85.7 %all-gather.4.cloned.1.call-done = bf16[512,8192]{1,0:T(8,128)(2,1)} async-done(((bf16[512,2048]{1,0:T(8,128)(2,1)}), bf16[512,8192]{1,0:T(8,128)(2,1)}) %all-gather.4.cloned.1.call-update) | async-done | bytes 8388624 | tf_op jit(solution)/shard_map/all_gather | solution.py:80
  308.5 24.9 %select_convert_fusion.1 = bf16[512,2048]{1,0:T(8,128)(2,1)} fusion(f32[512,2048]{1,0:T(8,128)} %fusion.17, bf16[512,8192]{1,0:T(8,128)(2,1)} %all-gather.4.cloned.1.call-done, bf16[8192,2048]{1,0:T(8,128)(2,1)} %param.10, pred[512]{0:T(512)(128)(4,1)S(1)} %broadcast_compare_fusion), kind=kOutput, calls=%fused_computation.21 | convolution fusion | flops 17183014912 | bytes 48235008 | tf_op jit(solution)/shard_map/dot_general | solution.py:94
  333.4 120.0 %reduce-scatter.2.cloned.1.call-done = bf16[512,2048]{1,0:T(8,128)(2,1)} async-done(((bf16[512,8192]{1,0:T(8,128)(2,1)}), bf16[512,2048]{1,0:T(8,128)(2,1)}) %reduce-scatter.2.cloned.1.call-update) | async-done | bytes 2097168 | tf_op jit(solution)/shard_map/reduce_scatter | solution.py:85
  453.4 10.3 %fusion.8 = bf16[512,2048]{1,0:T(8,128)(2,1)} fusion(f32[512,2048]{1,0:T(8,128)} %fusion.18, bf16[512,2048]{1,0:T(8,128)(2,1)} %reduce-scatter.2.cloned.1.call-done, bf16[512,2048]{1,0:T(8,128)(2,1)S(1)} %copy-done.3, bf16[8192,2048]{1,0:T(8,128)(2,1)} %param.10, s32[]{:T(128)S(6)} %select_n.140, pred[512]{0:T(512)(128)(4,1)S(1)} %broadcast_compare_fusion), kind=kOutput, calls=%fused_computation.18 | convolution fusion | flops 4300210176 | bytes 18874884 | tf_op jit(solution)/shard_map/dot_general | solution.py:87
  (76 shorter events, 8.6 us)
Async XLA Ops:
  7.2 51.1 %all-reduce.2.cloned.1.call-start = ((), (), s32[]{:S(2)}) async-start(), calls=%async_computation.2 | async-start | bytes 1048576 | tf_op jit(solution)/shard_map/psum | solution.py:77
  8.3 5.5 %copy-start.1 = (bf16[512,2048]{1,0:T(8,128)(2,1)S(1)}, bf16[512,2048]{1,0:T(8,128)(2,1)}, u32[]{:S(2)}) copy-start(bf16[512,2048]{1,0:T(8,128)(2,1)} %param.8) | copy-start | bytes 6291460
  8.3 5.5 %copy-start.8 = (bf16[2048,1024]{1,0:T(8,128)(2,1)S(1)}, bf16[2048,1024]{1,0:T(8,128)(2,1)}, u32[]{:S(2)}) copy-start(bf16[2048,1024]{1,0:T(8,128)(2,1)} %param.11) | copy-start | bytes 12582916
  13.8 3.4 copy-start.6
  13.8 3.4 copy-start.7
  17.1 90.9 %all-gather.6.cloned.1.call-start = ((), (), s32[]{:S(2)}) async-start(), calls=%async_computation.4 | async-start | bytes 1310720 | tf_op jit(solution)/shard_map/all_gather | solution.py:91
  18.9 44.9 %copy-start.2 = (bf16[512,2048]{1,0:T(8,128)(2,1)S(1)}, bf16[512,2048]{1,0:T(8,128)(2,1)}, u32[]{:S(2)}) copy-start(bf16[512,2048]{1,0:T(8,128)(2,1)} %param.8) | copy-start | bytes 6291460
  62.4 145.4 %all-gather.8.cloned.1.call-start = ((), (), s32[]{:S(2)}) async-start(), calls=%async_computation.5 | async-start | bytes 10485760 | tf_op jit(solution)/shard_map/all_gather | solution.py:90
  63.1 245.4 %all-gather.4.cloned.1.call-start = ((), (), s32[]{:S(2)}) async-start(), calls=%async_computation.1 | async-start | bytes 10485760 | tf_op jit(solution)/shard_map/all_gather | solution.py:80
  63.7 389.7 %reduce-scatter.2.cloned.1.call-start = ((), (), s32[]{:S(2)}) async-start(), calls=%async_computation.3 | async-start | bytes 10485760 | tf_op jit(solution)/shard_map/reduce_scatter | solution.py:85
  63.7 42.8 %collective-permute-start = (bf16[512,2048]{1,0:T(8,128)(2,1)S(1)}, bf16[512,2048]{1,0:T(8,128)(2,1)}, u32[]{:S(2)}, u32[]{:S(2)}) collective-permute-start(bf16[512,2048]{1,0:T(8,128)(2,1)S(1)} %copy-done.2), channel_id=1, source_target_pairs={{0,1},{1,2},{2,3},{3,0},{4,5},{5,6},{6,7},{7,4},{8,9},{9,10},{10,1... | collective-permute-start | bytes 6291464 | tf_op jit(solution)/shard_map/ppermute | solution.py:21
  89.0 0.7 copy-start.5
  94.8 7.3 %copy-start.9 = (bf16[2048,1024]{1,0:T(8,128)(2,1)S(1)}, bf16[2048,1024]{1,0:T(8,128)(2,1)}, u32[]{:S(2)}) copy-start(bf16[2048,1024]{1,0:T(8,128)(2,1)} %param.11) | copy-start | bytes 12582916
  106.6 56.2 %collective-permute-start.1 = (bf16[512,2048]{1,0:T(8,128)(2,1)}, bf16[512,2048]{1,0:T(8,128)(2,1)}, u32[]{:S(2)}, u32[]{:S(2)}) collective-permute-start(bf16[512,2048]{1,0:T(8,128)(2,1)} %collective-permute-done), channel_id=1, source_target_pairs={{0,1},{1,2},{2,3},{3,0},{4,5},{5,6},{6,7},{7,4},{8,9},{9,10},{10,1... | collective-permute-start | bytes 6291464 | tf_op jit(solution)/shard_map/ppermute | solution.py:21
  108.0 5.0 %copy-start = (bf16[2048,256]{1,0:T(8,128)(2,1)S(1)}, bf16[2048,256]{1,0:T(8,128)(2,1)}, u32[]{:S(2)}) copy-start(bf16[2048,256]{1,0:T(8,128)(2,1)} %all-gather.6.cloned.1.call-done) | copy-start | bytes 3145732
  113.8 49.9 %copy-start.4 = (bf16[2048,1024]{1,0:T(8,128)(2,1)}, bf16[2048,1024]{1,0:T(8,128)(2,1)S(1)}, u32[]{:S(2)}) copy-start(bf16[2048,1024]{1,0:T(8,128)(2,1)S(1)} %get-tuple-element.11) | copy-start | bytes 12582916
  162.8 25.7 %collective-permute-start.2 = (bf16[512,2048]{1,0:T(8,128)(2,1)}, bf16[512,2048]{1,0:T(8,128)(2,1)S(1)}, u32[]{:S(2)}, u32[]{:S(2)}) collective-permute-start(bf16[512,2048]{1,0:T(8,128)(2,1)} %collective-permute-done.1), channel_id=1, source_target_pairs={{0,1},{1,2},{2,3},{3,0},{4,5},{5,6},{6,7},{7,4},{8,9},{9,10},{10,1... | collective-permute-start | bytes 6291464 | tf_op jit(solution)/shard_map/ppermute | solution.py:21
  222.7 230.6 %copy-start.3 = (bf16[512,2048]{1,0:T(8,128)(2,1)S(1)}, bf16[512,2048]{1,0:T(8,128)(2,1)}, u32[]{:S(2)}) copy-start(bf16[512,2048]{1,0:T(8,128)(2,1)} %param.9) | copy-start | bytes 6291460
Sparse Core Ops, SparseCore 0:
  17.2 40.9 all-reduce.1
  62.5 19.5 all-gather.5
  83.7 73.6 all-gather.7
  158.7 149.6 all-gather.3
  310.7 142.6 reduce-scatter.1
